TPU v7x, 128 devices: a whole 4x4x4 slice. The times are simulated.
128 devices in a mesh: base: 16 (over z, y), freq: 8 (over x, core).
Axes of the slice: x: 4, y: 4, z: 4, core: 2. Of those that a mesh axis runs over, the one named last changes fastest.
Arguments:
- visibilities: bfloat16 [2, 16384, 2048], P(None, 'base', 'freq'), may hold values from -0.01171875 to 0.01171875
- anchor: bfloat16 [2, 16384], P(None, 'base'), may hold values from 4 to 60, as said below
- drift: bfloat16 [2, 16384], P(None, 'base'), may hold values from -0.01953125 to 0.01953125
- target: int32 [16384, 1], P('base'), may hold values from 0 to 127; in each aligned block of 1024 rows (0 to 1023, 1024 to 2047, ...) at most 8 rows name the same one
- subgrid_w: float32 [128], P('base'), may hold values from -1 to 1
- facet_owner: int32 [128, 1], P('base'), may hold values from 0 to 15; in each aligned block of 8 rows (0 to 7, 8 to 15, ...) at most 2 rows name the same one
- row_offset: int32 [128], P('base'), may hold values from 0 to 64
- col_offset: int32 [128], P('base'), may hold values from 0 to 16320
Outputs:
- grid: float32 [2, 2048, 16384], P(None, 'base')
Inputs may be any that keep to these rules, and one draw needn't show every extreme that they name: `target`: among the 1024 blocks of one index of base no subgrid is named more than 8 times. `facet_owner`: among the 8 subgrids of one index of base no owner is named more than 2 times. anchor[k,b] + 2048 drift[k,b] lies between 4 and 60, up to the rounding of drift.
All inputs are finite; a program needn't handle non-finite values.
Results may differ from a plain program's by a relative error of at most 0.0038.
Values may be sent and summed in bfloat16 or wider, within the bound.
A program may use at most 128 MiB of HBM per device.

v0:
```python
import math
import jax
import jax.numpy as jnp
from jax import lax
from jax.sharding import PartitionSpec as P

G = 64
GY = 16384
CAP = 8
FCAP = 2
FR = 128


def slot_table(target, groups, depth):
    total = target.shape[0]
    hits = (target[:, None] == jnp.arange(groups, dtype=jnp.int32)[None, :]).astype(jnp.int32)
    before = jnp.cumsum(hits, axis=0) - hits
    ranking = jnp.sum(before * hits, axis=1)
    placed = target * depth + ranking
    match = placed[None, :] == jnp.arange(groups * depth, dtype=jnp.int32)[:, None]
    source = jnp.sum(jnp.where(match, jnp.arange(total, dtype=jnp.int32)[None, :], 0), axis=1)
    filled = jnp.any(match, axis=1)
    return (source, filled)


def phase_table(start, slope, first, channels):
    pixels = (jnp.arange(G, dtype=jnp.int32) - G // 2).astype(jnp.float32) * (2.0 * math.pi / G)
    angles = jnp.concatenate([pixels, pixels])
    shifts = jnp.concatenate(
        [jnp.zeros((G,), jnp.float32), jnp.full((G,), -0.5 * math.pi, jnp.float32)]
    )
    coarse = (first + 16 * jnp.arange(channels // 16, dtype=jnp.int32)).astype(jnp.float32)
    fine = jnp.arange(16, dtype=jnp.int32).astype(jnp.float32)
    centre = start[:, None] + coarse[None, :] * slope[:, None] - 0.5 * G
    outer = centre[:, :, None] * angles + shifts
    inner = (fine[None, :] * slope[:, None])[:, :, None] * angles
    table = (
        jnp.cos(outer)[:, :, None, :] * jnp.cos(inner)[:, None, :, :]
        - jnp.sin(outer)[:, :, None, :] * jnp.sin(inner)[:, None, :, :]
    )
    return table.reshape(start.shape[0], channels, 2 * G)


def grid_one(data, where, first):
    bound = data.shape[1]
    channels = data.shape[2]
    values = where.astype(jnp.float32)
    left = (
        phase_table(values[0], values[2], first, channels)
        .astype(jnp.bfloat16)
        .reshape(bound * channels, 2 * G)
    )
    right = phase_table(values[1], values[3], first, channels)
    signs = jnp.concatenate([-jnp.ones((G,), jnp.float32), jnp.ones((G,), jnp.float32)])
    swapped = jnp.roll(right, G, axis=2) * signs
    real_part = data[0].astype(jnp.float32)[:, :, None]
    imag_part = data[1].astype(jnp.float32)[:, :, None]
    weighted = (
        (real_part * right + imag_part * swapped)
        .astype(jnp.bfloat16)
        .reshape(bound * channels, 2 * G)
    )
    product = lax.dot_general(
        left, weighted, (((0,), (0,)), ((), ())), preferred_element_type=jnp.float32
    )
    return jnp.stack([product[:G, :G] - product[G:, G:], product[:G, G:] + product[G:, :G]])


def to_patch(image, weight):
    axis_values = (jnp.arange(G, dtype=jnp.int32) - G // 2).astype(jnp.float32) / (0.5 * G)
    radius = axis_values[:, None] ** 2 + axis_values[None, :] ** 2
    phase = math.pi * weight[:, None, None] * radius
    cosine, sine = (jnp.cos(phase), jnp.sin(phase))
    kernel_real = image[:, 0] * cosine - image[:, 1] * sine
    kernel_imag = image[:, 0] * sine + image[:, 1] * cosine
    index = jnp.arange(G, dtype=jnp.int32)
    turns = (index[:, None] * index[None, :] % G).astype(jnp.float32) * (2.0 * math.pi / G)
    table_real, table_imag = (jnp.cos(turns), -jnp.sin(turns))
    highest = lax.Precision.HIGHEST

    def from_left(matrix, field):
        return jnp.einsum("jl,slm->sjm", matrix, field, precision=highest)

    def from_right(field, matrix):
        return jnp.einsum("sjm,km->sjk", field, matrix, precision=highest)

    turned_real = from_left(table_real, kernel_real) - from_left(table_imag, kernel_imag)
    turned_imag = from_left(table_real, kernel_imag) + from_left(table_imag, kernel_real)
    patch_real = from_right(turned_real, table_real) - from_right(turned_imag, table_imag)
    patch_imag = from_right(turned_real, table_imag) + from_right(turned_imag, table_real)
    return jnp.stack([patch_real, patch_imag], axis=1) * (1.0 / G)


def per_device(visibilities, anchor, drift, target, subgrid_w, facet_owner, row_offset, col_offset):
    base_count = lax.axis_size("base")
    own_subgrids = subgrid_w.shape[0]
    all_subgrids = own_subgrids * base_count
    channels = visibilities.shape[2]
    first = lax.axis_index("freq") * channels
    source, filled = slot_table(target[:, 0], all_subgrids, CAP)
    picked = jnp.where(
        filled[None, :, None], jnp.take(visibilities, source, axis=1), jnp.zeros((), jnp.bfloat16)
    )
    slotted = picked.reshape(2, all_subgrids, CAP, channels)
    places = jnp.concatenate([anchor, drift], axis=0)
    located = jnp.where(
        filled[None, :], jnp.take(places, source, axis=1), jnp.zeros((), jnp.bfloat16)
    )
    located = located.reshape(4, all_subgrids, CAP)
    grid_data = jnp.moveaxis(slotted, 1, 0)
    grid_where = jnp.moveaxis(located, 1, 0)

    def single(item):
        return grid_one(item[0], item[1], first)

    images = lax.psum_scatter(
        lax.map(single, (grid_data, grid_where)), "base", scatter_dimension=0, tiled=True
    )
    images = lax.psum(images, "freq")
    patches = to_patch(images, subgrid_w)
    chosen, kept = slot_table(facet_owner[:, 0], base_count, FCAP)
    flattened = patches.reshape(own_subgrids, 2 * G * G)
    outgoing = jnp.where(kept[:, None], jnp.take(flattened, chosen, axis=0), 0.0)
    spots = jnp.stack([row_offset, col_offset], axis=1).astype(jnp.float32)
    sent_spots = jnp.where(kept[:, None], jnp.take(spots, chosen, axis=0), 0.0)
    arrived, arrived_spots = (
        lax.all_to_all(outgoing, "base", split_axis=0, concat_axis=0, tiled=True),
        lax.all_to_all(sent_spots, "base", split_axis=0, concat_axis=0, tiled=True),
    )
    corners = arrived_spots.astype(jnp.int32)

    def deposit(position, facet):
        start = (jnp.zeros((), jnp.int32), corners[position, 0], corners[position, 1])
        region = lax.dynamic_slice(facet, start, (2, G, G))
        patch = arrived[position].reshape(2, G, G)
        return lax.dynamic_update_slice(facet, region + patch, start)

    return lax.fori_loop(0, arrived.shape[0], deposit, jnp.zeros((2, FR, GY), jnp.float32))


def solution(mesh):
    return jax.shard_map(
        per_device,
        mesh=mesh,
        in_specs=(
            P(None, "base", "freq"),
            P(None, "base"),
            P(None, "base"),
            P("base", None),
            P("base"),
            P("base", None),
            P("base"),
            P("base"),
        ),
        out_specs=P(None, "base", None),
        check_vma=False,
    )
```

profile of v0, /device:TPU:23, one launch (start us, length us, event | category | flops | bytes accessed | tf_op | source)
XLA Modules:
  0.0 998.7 jit_solution(2251787866545427747)
XLA Ops:
  11.7 3.2 gather_fusion.1
  15.9 5.3 gather_fusion.2
  21.9 490.5 %while.26 = (s32[]{:T(128)}, f32[128,2,64,64]{3,2,1,0:T(8,128)}, bf16[128,4,8]{2,1,0:T(4,128)(2,1)S(1)}, s32[]{:T(128)}, bf16[128,2,8,256]{3,2,0,1:T(8,128)(2,1)...) while((s32[]{:T(128)}, f32[128,2,64,64]{3,2,1,0:T(8,128)}, bf16[128,4,8]{2,1,0:T(4,128)(2,1)S(1)}, ...), condition=%wide.region_10.11_spmd, body=%wide.region_9.10_spmd.sunk | while | flops 71423392 | bytes 5864877 | solution.py:117
  81.2 1.2 convolution_bitcast_fusion.2
  515.2 7.7 all-to-all-start
  523.2 74.6 %reduce-scatter.2.cloned.1.call-done = f32[8,2,64,64]{3,2,1,0:T(8,128)} async-done(((f32[128,2,64,64]{3,2,1,0:T(8,128)}), f32[8,2,64,64]{3,2,1,0:T(8,128)}) %reduce-scatter.2.cloned.1.call-update) | async-done | bytes 262160 | tf_op jit(solution)/shard_map/reduce_scatter | solution.py:116
  597.8 62.8 %all-reduce.2.cloned.1.call-done = f32[8,2,64,64]{3,2,1,0:T(8,128)} async-done(((f32[8,2,64,64]{3,2,1,0:T(8,128)}), f32[8,2,64,64]{3,2,1,0:T(8,128)}) %all-reduce.2.cloned.1.call-update) | async-done | bytes 262160 | tf_op jit(solution)/shard_map/psum | solution.py:119
  660.6 2.7 fusion.50
  663.3 2.7 fusion.23
  667.3 2.7 fusion.46
  670.0 2.7 fusion.22
  675.8 1.7 select_select_fusion
  677.5 6.9 all-to-all-start.1
  684.6 15.4 %all-to-all-done.1 = f32[16,2,8192]{2,1,0:T(2,128)S(1)} async-done(((f32[16,2,8192]{2,1,0:T(2,128)}), f32[16,2,8192]{2,1,0:T(2,128)S(1)}, u32[]{:S(2)}, u32[]{:S(2)}) %all-to-all-start.1) | async-done | bytes 1048608 | tf_op jit(solution)/shard_map/all_to_all | solution.py:127
  700.8 8.1 broadcast_in_dim.170
  708.9 283.0 %while.27 = (s32[]{:T(128)}, f32[2,128,16384]{2,1,0:T(8,128)}, s32[32,2]{0,1:T(2,128)S(1)}, f32[32,8192]{1,0:T(8,128)S(1)}, s32[]{:T(128)}, /*index=5*/s32[]{:T(128)}, s32[]{:T(128)}, s32[]{:T(128)}) while((s32[]{:T(128)}, f32[2,128,16384]{2,1,0:T(8,128)}, s32[32,2]{0,1:T(2,128)S(1)}, f32[32,8192]{1,0:T(8,128)S(1)}, s32[]{:T(128)}, ...), condition=%wide.region_14.15_spmd, body=%wide.region_13.14_spmd.sunk | while | flops 8200 | bytes 295109 | solution.py:138
  714.5 3.4 dynamic_update_slice.19
  723.4 3.4 dynamic_update_slice.19
  732.4 3.4 dynamic_update_slice.19
  741.4 3.3 dynamic_update_slice.19
  750.2 3.3 dynamic_update_slice.19
  759.1 3.3 dynamic_update_slice.19
  768.0 3.3 dynamic_update_slice.19
  776.9 3.3 dynamic_update_slice.19
  785.8 3.3 dynamic_update_slice.19
  794.7 3.3 dynamic_update_slice.19
  803.5 2.6 dynamic_update_slice.19
  811.8 3.3 dynamic_update_slice.19
  820.7 3.3 dynamic_update_slice.19
  829.6 3.2 dynamic_update_slice.19
  838.4 2.2 dynamic_update_slice.19
  846.2 3.4 dynamic_update_slice.19
  855.1 3.3 dynamic_update_slice.19
  864.1 3.3 dynamic_update_slice.19
  873.0 3.3 dynamic_update_slice.19
  881.9 3.3 dynamic_update_slice.19
  890.8 3.3 dynamic_update_slice.19
  899.7 3.3 dynamic_update_slice.19
  908.6 3.3 dynamic_update_slice.19
  917.5 3.3 dynamic_update_slice.19
  926.4 3.3 dynamic_update_slice.19
  935.3 3.2 dynamic_update_slice.19
  944.1 3.4 dynamic_update_slice.19
  953.1 3.2 dynamic_update_slice.19
  961.9 3.4 dynamic_update_slice.19
  970.9 3.3 dynamic_update_slice.19
  979.8 3.3 dynamic_update_slice.19
  988.7 3.2 dynamic_update_slice.19
  (2251 shorter events, 554.8 us)
Async XLA Ops:
  6.5 9.4 copy-start
  6.5 15.3 %copy-start.6 = (f32[128]{0:T(128)S(1)}, f32[128]{0:T(128)}, u32[]{:S(2)}) copy-start(f32[128]{0:T(128)} %constant.174.clone.1) | copy-start | bytes 1540
  6.5 15.3 %copy-start.1 = (f32[128]{0:T(128)S(1)}, f32[128]{0:T(128)}, u32[]{:S(2)}) copy-start(f32[128]{0:T(128)} %constant.173.clone.1) | copy-start | bytes 1540
  6.5 591.3 %reduce-scatter.2.cloned.1.call-start = ((), (), s32[]{:S(2)}) async-start(), calls=%async_computation.3 | async-start | bytes 8912896 | tf_op jit(solution)/shard_map/reduce_scatter | solution.py:116
  512.3 0.7 copy-start.3
  512.3 0.7 copy-start.4
  512.3 0.8 copy-start.2
  512.3 85.5 %copy-start.5 = (f32[8]{0:T(128)S(1)}, f32[8]{0:T(128)}, u32[]{:S(2)}) copy-start(f32[8]{0:T(128)} %param.16) | copy-start | bytes 100
  515.2 162.3 %all-to-all-start = ((f32[16,2,2]{1,2,0:T(2,128)}), f32[16,2,2]{1,2,0:T(2,128)S(1)}, u32[]{:S(2)}, u32[]{:S(2)}) async-start(f32[16,2,2]{1,2,0:T(2,128)} %copy.84), calls=%async_computation | async-start | bytes 32768 | tf_op jit(solution)/shard_map/all_to_all | solution.py:128
  522.9 137.7 %all-reduce.2.cloned.1.call-start = ((), (), s32[]{:S(2)}) async-start(), calls=%async_computation.4 | async-start | bytes 1048576 | tf_op jit(solution)/shard_map/psum | solution.py:119
  677.5 22.5 %all-to-all-start.1 = ((f32[16,2,8192]{2,1,0:T(2,128)}), f32[16,2,8192]{2,1,0:T(2,128)S(1)}, u32[]{:S(2)}, u32[]{:S(2)}) async-start(f32[16,2,8192]{2,1,0:T(2,128)} %select_select_fusion), calls=%async_computation.2 | async-start | bytes 2097152 | tf_op jit(solution)/shard_map/all_to_all | solution.py:127
Sparse Core Ops, SparseCore 0:
  512.5 85.2 reduce-scatter.1
  600.1 60.4 all-reduce.1
where the time goes:
time: 1010 us; the launch traced here: 999 us
  other arithmetic  298 us (30%)
  local copies, waits for them, and re-layouts  220 us (22%)
  matrix products  171 us (17%)
  waiting for transfers between devices  153 us (15%)
  loops' own time  129 us (13%)
  starting transfers between devices  14.8 us (1%)
  between operations  13.7 us (1%)
    dot_general x128, matrix products, grid_one(): lax.dot_general(left, weighted, (((0,), (0,)), ((), ())), preferred_eleme...  158 us
    cos x128, other arithmetic, phase_table(): jnp.cos(outer)[:, :, None, :] * jnp.cos(inner)[:, None, :, :]  126 us
    another operation x1, loops' own time, per_device(): lax.fori_loop(0, arrived.shape[0], deposit, jnp.zeros((2, FR, GY), jnp.fl...  121 us
    dynamic_update_slice x32, local copies, waits for them, and re-layouts, deposit(): return lax.dynamic_update_slice(facet, region + patch, start)  104 us
    dynamic_update_slice x128, other arithmetic, per_device(): lax.map(single, (grid_data, grid_where))  82.3 us
    reduce_scatter x1, waiting for transfers between devices, per_device(): lax.psum_scatter(lax.map(single, (grid_data, grid_where)), 'base', scatte...  74.6 us
    psum x1, waiting for transfers between devices, per_device(): images = lax.psum(images, 'freq')  62.8 us
    slice x128, local copies, waits for them, and re-layouts, grid_one(): swapped = jnp.roll(right, G, axis=2) * signs  44.2 us
  transfers between devices with their start and end apart: 4, of which 3 were waited for; matrix products, arithmetic and copies ran while one was open for 2% of the time, Pallas kernels for 0%

commit v1 on v0

--- a/solution.py
+++ b/solution.py
@@ -116,7 +116,12 @@
     images = lax.psum_scatter(
         lax.map(single, (grid_data, grid_where)), "base", scatter_dimension=0, tiled=True
     )
-    images = lax.psum(images, "freq")
+    count = lax.axis_size("freq")
+    result, hop = (images, 1)
+    while hop < count:
+        result = result + lax.ppermute(result, "freq", [(i, i ^ hop) for i in range(count)])
+        hop = 2 * hop
+    images = result
     patches = to_patch(images, subgrid_w)
     chosen, kept = slot_table(facet_owner[:, 0], base_count, FCAP)
     flattened = patches.reshape(own_subgrids, 2 * G * G)

time: 1010 us -> 970 us (0.960)
  waiting for transfers between devices: 153 us -> 117 us
    psum x1 -> x0, waiting for transfers between devices: 62.8 us -> none  [per_device(): images = lax.psum(images, 'freq')]
    ppermute x0 -> x3, waiting for transfers between devices: none -> 20 us  [per_device(): lax.ppermute(result, 'freq', [(i, i ^ hop) for i in range(count)])]
  transfers between devices with their start and end apart: 4 -> 6, of which waited for: 3 -> 5; matrix products, arithmetic and copies ran while one was open for 2% -> 2% of each run, Pallas kernels for 0% -> 0%
where the time goes in v1:
time: 970 us; the launch traced here: 960 us
  other arithmetic  299 us (31%)
  local copies, waits for them, and re-layouts  220 us (23%)
  matrix products  167 us (17%)
  loops' own time  129 us (13%)
  waiting for transfers between devices  117 us (12%)
  starting transfers between devices  14.7 us (2%)
  between operations  13.7 us (1%)
    dot_general x128, matrix products, grid_one(): lax.dot_general(left, weighted, (((0,), (0,)), ((), ())), preferred_eleme...  158 us
    cos x128, other arithmetic, phase_table(): jnp.cos(outer)[:, :, None, :] * jnp.cos(inner)[:, None, :, :]  126 us
    another operation x1, loops' own time, per_device(): lax.fori_loop(0, arrived.shape[0], deposit, jnp.zeros((2, FR, GY), jnp.fl...  121 us
    dynamic_update_slice x32, local copies, waits for them, and re-layouts, deposit(): return lax.dynamic_update_slice(facet, region + patch, start)  104 us
    reduce_scatter x1, waiting for transfers between devices, per_device(): lax.psum_scatter(lax.map(single, (grid_data, grid_where)), 'base', scatte...  84.2 us
    dynamic_update_slice x128, other arithmetic, per_device(): lax.map(single, (grid_data, grid_where))  82.3 us
    slice x128, local copies, waits for them, and re-layouts, grid_one(): swapped = jnp.roll(right, G, axis=2) * signs  44.2 us
    add x32, other arithmetic, deposit(): return lax.dynamic_update_slice(facet, region + patch, start)  32 us
  transfers between devices with their start and end apart: 6, of which 5 were waited for; matrix products, arithmetic and copies ran while one was open for 2% of the time, Pallas kernels for 0%

profile of v1, /device:TPU:23, one launch (start us, length us, event | category | flops | bytes accessed | tf_op | source)
XLA Modules:
  0.0 959.5 jit_solution(12612622093094507442)
XLA Ops:
  11.7 3.2 gather_fusion.1
  15.9 5.3 gather_fusion.2
  21.9 490.5 %while.26 = (s32[]{:T(128)}, f32[128,2,64,64]{3,2,1,0:T(8,128)}, bf16[128,4,8]{2,1,0:T(4,128)(2,1)S(1)}, s32[]{:T(128)}, bf16[128,2,8,256]{3,2,0,1:T(8,128)(2,1)...) while((s32[]{:T(128)}, f32[128,2,64,64]{3,2,1,0:T(8,128)}, bf16[128,4,8]{2,1,0:T(4,128)(2,1)S(1)}, ...), condition=%wide.region_10.11_spmd, body=%wide.region_9.10_spmd.sunk | while | flops 71423392 | bytes 5864877 | solution.py:117
  513.5 84.2 %reduce-scatter.2.cloned.1.call-done = f32[8,2,64,64]{3,2,1,0:T(8,128)} async-done(((f32[128,2,64,64]{3,2,1,0:T(8,128)}), f32[8,2,64,64]{3,2,1,0:T(8,128)}) %reduce-scatter.2.cloned.1.call-update) | async-done | bytes 262160 | tf_op jit(solution)/shard_map/reduce_scatter | solution.py:116
  597.7 2.4 collective-permute-start
  604.0 5.2 all-to-all-start
  609.3 6.8 collective-permute-done.1
  617.6 12.5 %collective-permute-done.2 = f32[8,2,64,64]{3,2,1,0:T(8,128)S(1)} collective-permute-done((f32[8,2,64,64]{3,2,1,0:T(8,128)S(1)}, f32[8,2,64,64]{3,2,1,0:T(8,128)S(1)}, u32[]{:S(2)}, u32[]{:S(2)}) %collective-permute-start.2) | collective-permute-done | bytes 262176 | tf_op jit(solution)/shard_map/ppermute | solution.py:122
  631.9 1.7 fusion.50
  633.6 1.7 fusion.23
  636.5 1.7 fusion.22
  641.3 1.7 select_select_fusion
  643.0 5.1 all-to-all-start.1
  648.4 12.4 %all-to-all-done.1 = f32[16,2,8192]{2,1,0:T(2,128)S(1)} async-done(((f32[16,2,8192]{2,1,0:T(2,128)}), f32[16,2,8192]{2,1,0:T(2,128)S(1)}, u32[]{:S(2)}, u32[]{:S(2)}) %all-to-all-start.1) | async-done | bytes 1048608 | tf_op jit(solution)/shard_map/all_to_all | solution.py:132
  661.5 8.1 broadcast_in_dim.170
  669.7 283.0 %while.27 = (s32[]{:T(128)}, f32[2,128,16384]{2,1,0:T(8,128)}, s32[32,2]{0,1:T(2,128)S(1)}, f32[32,8192]{1,0:T(8,128)S(1)}, s32[]{:T(128)}, /*index=5*/s32[]{:T(128)}, s32[]{:T(128)}, s32[]{:T(128)}) while((s32[]{:T(128)}, f32[2,128,16384]{2,1,0:T(8,128)}, s32[32,2]{0,1:T(2,128)S(1)}, f32[32,8192]{1,0:T(8,128)S(1)}, s32[]{:T(128)}, ...), condition=%wide.region_13.14_spmd, body=%wide.region_12.13_spmd.sunk | while | flops 8200 | bytes 295109 | solution.py:143
  675.3 3.4 dynamic_update_slice.19
  684.2 3.4 dynamic_update_slice.19
  693.2 3.4 dynamic_update_slice.19
  702.1 3.3 dynamic_update_slice.19
  711.0 3.3 dynamic_update_slice.19
  719.9 3.3 dynamic_update_slice.19
  728.8 3.3 dynamic_update_slice.19
  737.6 3.3 dynamic_update_slice.19
  746.5 3.3 dynamic_update_slice.19
  755.5 3.3 dynamic_update_slice.19
  764.3 2.6 dynamic_update_slice.19
  772.6 3.3 dynamic_update_slice.19
  781.5 3.3 dynamic_update_slice.19
  790.3 3.2 dynamic_update_slice.19
  799.1 2.2 dynamic_update_slice.19
  807.0 3.4 dynamic_update_slice.19
  815.9 3.3 dynamic_update_slice.19
  824.8 3.3 dynamic_update_slice.19
  833.8 3.3 dynamic_update_slice.19
  842.7 3.3 dynamic_update_slice.19
  851.6 3.3 dynamic_update_slice.19
  860.5 3.3 dynamic_update_slice.19
  869.3 3.3 dynamic_update_slice.19
  878.3 3.3 dynamic_update_slice.19
  887.2 3.3 dynamic_update_slice.19
  896.1 3.2 dynamic_update_slice.19
  904.9 3.4 dynamic_update_slice.19
  913.9 3.2 dynamic_update_slice.19
  922.7 3.4 dynamic_update_slice.19
  931.7 3.3 dynamic_update_slice.19
  940.5 3.3 dynamic_update_slice.19
  949.4 3.2 dynamic_update_slice.19
  (2257 shorter events, 561.3 us)
Async XLA Ops:
  6.5 9.4 copy-start
  6.5 15.3 %copy-start.6 = (f32[128]{0:T(128)S(1)}, f32[128]{0:T(128)}, u32[]{:S(2)}) copy-start(f32[128]{0:T(128)} %constant.174.clone.1) | copy-start | bytes 1540
  6.5 15.3 %copy-start.1 = (f32[128]{0:T(128)S(1)}, f32[128]{0:T(128)}, u32[]{:S(2)}) copy-start(f32[128]{0:T(128)} %constant.173.clone.1) | copy-start | bytes 1540
  6.5 591.1 %reduce-scatter.2.cloned.1.call-start = ((), (), s32[]{:S(2)}) async-start(), calls=%async_computation.3 | async-start | bytes 8912896 | tf_op jit(solution)/shard_map/reduce_scatter | solution.py:116
  512.3 0.7 copy-start.2
  512.3 87.7 %copy-start.3 = (s32[8]{0:T(128)S(1)}, s32[8]{0:T(128)}, u32[]{:S(2)}) copy-start(s32[8]{0:T(128)} %param.19) | copy-start | bytes 100
  512.3 87.7 %copy-start.4 = (s32[8]{0:T(128)S(1)}, s32[8]{0:T(128)}, u32[]{:S(2)}) copy-start(s32[8]{0:T(128)} %param.18) | copy-start | bytes 100
  512.3 97.0 %copy-start.5 = (f32[8]{0:T(128)S(1)}, f32[8]{0:T(128)}, u32[]{:S(2)}) copy-start(f32[8]{0:T(128)} %param.16) | copy-start | bytes 100
  597.7 4.1 collective-permute-start
  602.9 13.2 %collective-permute-start.1 = (f32[8,2,64,64]{3,2,1,0:T(8,128)S(1)}, f32[8,2,64,64]{3,2,1,0:T(8,128)S(1)}, u32[]{:S(2)}, u32[]{:S(2)}) collective-permute-start(f32[8,2,64,64]{3,2,1,0:T(8,128)S(1)} %add.333), channel_id=1, source_target_pairs={{0,2},{1,3},{2,0},{3,1},{4,6},{5,7},{6,4},{7,5},{8,10},{9,11},{10,... | collective-permute-start | bytes 786440 | tf_op jit(solution)/shard_map/ppermute | solution.py:122
  604.0 39.0 %all-to-all-start = ((f32[16,2,2]{1,2,0:T(2,128)}), f32[16,2,2]{1,2,0:T(2,128)S(1)}, u32[]{:S(2)}, u32[]{:S(2)}) async-start(f32[16,2,2]{1,2,0:T(2,128)} %copy.84), calls=%async_computation | async-start | bytes 32768 | tf_op jit(solution)/shard_map/all_to_all | solution.py:133
  616.2 14.0 %collective-permute-start.2 = (f32[8,2,64,64]{3,2,1,0:T(8,128)S(1)}, f32[8,2,64,64]{3,2,1,0:T(8,128)S(1)}, u32[]{:S(2)}, u32[]{:S(2)}) collective-permute-start(f32[8,2,64,64]{3,2,1,0:T(8,128)S(1)} %add.334), channel_id=1, source_target_pairs={{0,4},{1,5},{2,6},{3,7},{4,0},{5,1},{6,2},{7,3},{8,12},{9,13},{10,... | collective-permute-start | bytes 786440 | tf_op jit(solution)/shard_map/ppermute | solution.py:122
  643.0 17.8 %all-to-all-start.1 = ((f32[16,2,8192]{2,1,0:T(2,128)}), f32[16,2,8192]{2,1,0:T(2,128)S(1)}, u32[]{:S(2)}, u32[]{:S(2)}) async-start(f32[16,2,8192]{2,1,0:T(2,128)} %select_select_fusion), calls=%async_computation.2 | async-start | bytes 2097152 | tf_op jit(solution)/shard_map/all_to_all | solution.py:132
Sparse Core Ops, SparseCore 0:
  512.5 85.1 reduce-scatter.1
